TPU v7x, 32 devices: a whole 2x2x4 slice. The times are simulated.
32 devices in a mesh: groups: 2 (over y), ctx: 4 (over z), tensor: 2 (over x), dp: 2 (over core).
Axes of the slice: x: 2, y: 2, z: 4, core: 2. Of those that a mesh axis runs over, the one named last changes fastest.
Arguments:
- tokens: bfloat16 [4, 1024, 1024], P(('groups', 'dp'), 'ctx', 'tensor'), parts along dimension 0
- w_qkv: bfloat16 [1024, 3, 1024], P(None, None, 'tensor')
- w_out: bfloat16 [1024, 1024], P('tensor'), may hold values from -0.1875 to 0.1875
- labels: int32 [4, 8, 1024], P(('groups', 'dp'), 'tensor', 'ctx'), parts along dimension 0, may hold values from 0 to 255, as said below
- grad_out: bfloat16 [4, 1024, 1024], P(('groups', 'dp'), 'ctx', 'tensor'), parts along dimension 0, may hold values from -6 to 6
Outputs:
- attended: bfloat16 [4, 1024, 1024], P(('groups', 'dp'), 'ctx', 'tensor'), parts along dimension 0
- grad_tokens: bfloat16 [4, 1024, 1024], P(('groups', 'dp'), 'ctx', 'tensor'), parts along dimension 0
- grad_w_qkv: float32 [2048, 3, 1024], P('groups', None, 'tensor'), parts along dimension 0
- grad_w_out: float32 [2048, 1024], P(('groups', 'tensor')), parts along dimension 0
There are 2 independent parts, one for each index of `groups`. A program takes and returns all parts, laid end to end along the dimension named above; an argument that names none is the same for every part. Nothing has to cross between parts.
Inputs may be any that keep to these rules, and one draw needn't show every extreme that they name: `labels`: cluster c of any head belongs to owner c % 4. Among the 256 tokens of one document on one index of ctx, at most 192 have, for one head, clusters of one owner; for each head one owner has exactly 192 from every such block, and the other owners share the rest of a block evenly (counts differ by at most one).
All inputs are finite; a program needn't handle non-finite values.
Results may differ from a plain program's by a relative error of at most 0.035.
The roundings to bfloat16 on the way count: a program that leaves them out, or rounds other values in their place, can miss the bound.
Values may be sent and summed in bfloat16 or wider, within the bound.
A program may use at most 64 MiB of HBM per device.

v0:
```python
import math
import jax
import jax.numpy as jnp
from jax import lax
from jax.sharding import PartitionSpec as P

HD = 128


def contract_last(left, right):
    return lax.dot_general(
        left, right, (((1,), (1,)), ((), ())), preferred_element_type=jnp.float32
    )


def contract_first(left, right):
    return lax.dot_general(
        left, right, (((0,), (0,)), ((), ())), preferred_element_type=jnp.float32
    )


def masked_probs(query_block, label_block, keys_in, marks):
    scores = contract_last(query_block, keys_in) * HD ** (-0.5)
    same = label_block[:, None] == marks[None, :]
    scores = jnp.where(same, scores, jnp.float32(-1e30))
    top_value = jnp.max(scores, axis=1, keepdims=True)
    expo = jnp.exp(scores - top_value)
    return expo / jnp.sum(expo, axis=1, keepdims=True)


def owner_forward(queries, keys_in, values_in, marks):
    total = queries.shape[0]
    block_rows = math.gcd(total, 512)
    block_count = total // block_rows

    def forward_block(index):
        start = index * block_rows
        query_block = lax.dynamic_slice_in_dim(queries, start, block_rows, 0)
        label_block = lax.dynamic_slice_in_dim(marks, start, block_rows, 0)
        probs = masked_probs(query_block, label_block, keys_in, marks).astype(jnp.bfloat16)
        return jnp.dot(probs, values_in, preferred_element_type=jnp.float32).astype(jnp.bfloat16)

    return lax.map(forward_block, jnp.arange(block_count, dtype=jnp.int32)).reshape(
        total, queries.shape[1]
    )


def owner_backward(queries, keys_in, values_in, marks, attention, cotangent):
    total, size = queries.shape
    block_rows = math.gcd(total, 512)
    block_count = total // block_rows

    def backward_block(carry, index):
        grad_keys, grad_values = carry
        start = index * block_rows
        query_block = lax.dynamic_slice_in_dim(queries, start, block_rows, 0)
        label_block = lax.dynamic_slice_in_dim(marks, start, block_rows, 0)
        attn_block = lax.dynamic_slice_in_dim(attention, start, block_rows, 0)
        cot_block = lax.dynamic_slice_in_dim(cotangent, start, block_rows, 0)
        probs_full = masked_probs(query_block, label_block, keys_in, marks)
        probs = probs_full.astype(jnp.bfloat16)
        dprob = contract_last(cot_block, values_in)
        delta = jnp.sum(
            cot_block.astype(jnp.float32) * attn_block.astype(jnp.float32), axis=1, keepdims=True
        )
        dscore = (probs_full * (dprob - delta) * HD ** (-0.5)).astype(jnp.bfloat16)
        grad_query = jnp.dot(dscore, keys_in, preferred_element_type=jnp.float32).astype(
            jnp.bfloat16
        )
        grad_keys = grad_keys + contract_first(dscore, query_block)
        grad_values = grad_values + contract_first(probs, cot_block)
        return ((grad_keys, grad_values), grad_query)

    empty = jnp.zeros((total, size), jnp.float32)
    (grad_keys, grad_values), grad_queries = lax.scan(
        backward_block, (empty, empty), jnp.arange(block_count, dtype=jnp.int32)
    )
    return (
        grad_queries.reshape(total, size),
        grad_keys.astype(jnp.bfloat16),
        grad_values.astype(jnp.bfloat16),
    )


def shards(tokens, w_qkv, w_out, labels, grad_out):
    rows_all, grads_all = (
        lax.all_gather(tokens, "tensor", axis=2, tiled=True),
        lax.all_gather(grad_out, "tensor", axis=2, tiled=True),
    )
    tok_rows = rows_all[0]
    tok_grads = grads_all[0]
    tok_count, width = tok_rows.shape
    heads_local = w_out.shape[0] // HD
    ctx_count = lax.axis_size("ctx")
    capacity = 3 * tok_count // ctx_count
    slot_total = ctx_count * capacity
    qkv = jnp.dot(
        tok_rows, w_qkv.reshape(width, 3 * heads_local * HD), preferred_element_type=jnp.float32
    )
    qkv = qkv.astype(jnp.bfloat16).reshape(tok_count, 3, heads_local, HD)
    qkv_heads = jnp.transpose(qkv, (2, 0, 1, 3)).reshape(heads_local, tok_count, 3 * HD)
    cotangent = contract_last(tok_grads, w_out).astype(jnp.bfloat16)
    cot_heads = jnp.transpose(cotangent.reshape(tok_count, heads_local, HD), (1, 0, 2))
    labels_local = labels[0]
    owner_of = labels_local % ctx_count
    owner_hits = (
        owner_of[:, :, None] == jnp.arange(ctx_count, dtype=jnp.int32)[None, None, :]
    ).astype(jnp.int32)
    earlier = jnp.cumsum(owner_hits, axis=1) - owner_hits
    slot_index = jnp.sum(earlier * owner_hits, axis=2)
    destination = owner_of * capacity + slot_index

    def pack(values):
        feature_count = values.shape[2]
        empty_buffer = jnp.zeros((heads_local, slot_total, feature_count), values.dtype)
        filled = jax.vmap(lambda buffer, where_to, rows_in: buffer.at[where_to].set(rows_in))(
            empty_buffer, destination, values
        )
        return filled.reshape(heads_local, ctx_count, capacity, feature_count)

    def unpack(received):
        flat = received.reshape(heads_local, slot_total, received.shape[3])
        return jax.vmap(lambda table, where_to: jnp.take(table, where_to, axis=0))(
            flat, destination
        )

    label_slots = jax.vmap(
        lambda where_to, marks: jnp.full((slot_total,), -1.0, jnp.bfloat16).at[where_to].set(marks)
    )(destination, labels_local.astype(jnp.bfloat16)).reshape(heads_local, ctx_count, capacity)
    arrived, arrived_marks = (
        lax.all_to_all(pack(qkv_heads), "ctx", split_axis=1, concat_axis=1, tiled=True),
        lax.all_to_all(label_slots, "ctx", split_axis=1, concat_axis=1, tiled=True),
    )
    arrived = arrived.reshape(heads_local, slot_total, 3 * HD)
    marks_own = arrived_marks.reshape(heads_local, slot_total)
    queries_own = arrived[:, :, :HD]
    keys_own = arrived[:, :, HD : 2 * HD]
    values_own = arrived[:, :, 2 * HD :]
    attention_own = jax.vmap(owner_forward)(queries_own, keys_own, values_own, marks_own)
    returned = lax.all_to_all(
        attention_own.reshape(heads_local, ctx_count, capacity, HD),
        "ctx",
        split_axis=1,
        concat_axis=1,
        tiled=True,
    )
    attention_tok = unpack(returned)
    cot_arrived = lax.all_to_all(pack(cot_heads), "ctx", split_axis=1, concat_axis=1, tiled=True)
    cot_own = cot_arrived.reshape(heads_local, slot_total, HD)
    grad_q, grad_k, grad_v = jax.vmap(owner_backward)(
        queries_own, keys_own, values_own, marks_own, attention_own, cot_own
    )
    grads_own = jnp.concatenate([grad_q, grad_k, grad_v], axis=2).reshape(
        heads_local, ctx_count, capacity, 3 * HD
    )
    grads_back = lax.all_to_all(grads_own, "ctx", split_axis=1, concat_axis=1, tiled=True)
    grad_heads = unpack(grads_back)
    attention_rows = jnp.transpose(attention_tok, (1, 0, 2)).reshape(tok_count, heads_local * HD)
    out_terms = jnp.dot(attention_rows, w_out, preferred_element_type=jnp.float32)
    attended = lax.psum_scatter(
        out_terms.astype(jnp.bfloat16), "tensor", scatter_dimension=1, tiled=True
    )
    grad_qkv = jnp.transpose(grad_heads.reshape(heads_local, tok_count, 3, HD), (1, 2, 0, 3))
    grad_qkv = grad_qkv.reshape(tok_count, 3 * heads_local * HD)
    grad_w_out_local = contract_first(attention_rows, tok_grads)
    grad_w_qkv_local = contract_first(tok_rows, grad_qkv).reshape(width, 3, heads_local * HD)
    summed_qkv, summed_out = (
        lax.psum(grad_w_qkv_local.astype(jnp.bfloat16), ("ctx", "dp")).astype(jnp.float32),
        lax.psum(grad_w_out_local.astype(jnp.bfloat16), ("ctx", "dp")).astype(jnp.float32),
    )
    in_terms = contract_last(grad_qkv, w_qkv.reshape(width, 3 * heads_local * HD))
    grad_tokens = lax.psum_scatter(
        in_terms.astype(jnp.bfloat16), "tensor", scatter_dimension=1, tiled=True
    )
    return (attended[None], grad_tokens[None], summed_qkv, summed_out)


def solution(mesh):
    placed = (
        P(("groups", "dp"), "ctx", "tensor"),
        P(None, None, "tensor"),
        P("tensor", None),
        P(("groups", "dp"), "tensor", "ctx"),
        P(("groups", "dp"), "ctx", "tensor"),
    )
    return jax.shard_map(
        shards,
        mesh=mesh,
        in_specs=placed,
        out_specs=(
            P(("groups", "dp"), "ctx", "tensor"),
            P(("groups", "dp"), "ctx", "tensor"),
            P("groups", None, "tensor"),
            P(("groups", "tensor"), None),
        ),
        check_vma=False,
    )
```

profile of v0, /device:TPU:0, one launch (start us, length us, event | category | flops | bytes accessed | tf_op | source)
XLA Modules:
  0.0 419.2 jit_solution(18375576288930993019)
XLA Ops:
  10.2 4.8 %reduce-window.6 = s32[4,4,2,128]{3,2,1,0:T(2,128)S(1)} reduce-window(s32[4,4,2,128]{3,2,1,0:T(2,128)S(1)} %compare_convert_fusion, s32[]{:T(128)} %constant.96.clone.1), window={size=1x1x1x128 pad=0_0x0_0x0_0x127_0}, to_apply=%region_0.1 | reduce-window | flops 520192 | bytes 32772 | tf_op jit(solution)/shard_map/reduce-window
  17.8 7.6 %scatter_custom_fusion = bf16[3072]{0:T(1024)(128)(2,1)S(1)} fusion(s32[1024]{0:T(1024)S(1)} %bitcast.228, bf16[1024]{0:T(1024)(128)(2,1)S(1)} %bitcast.231, bf16[]{:T(256)} %constant.103.clone.1), kind=kCustom, calls=%fused_computation.120 | custom fusion | bytes 6146
  26.1 6.3 %all-to-all-start = ((bf16[4,4,192]{2,0,1:T(4,128)(2,1)}), bf16[4,4,192]{2,0,1:T(4,128)(2,1)S(1)}, u32[]{:S(2)}, u32[]{:S(2)}) async-start(bf16[4,4,192]{2,0,1:T(4,128)(2,1)} %copy.67), calls=%async_computation | async-start | bytes 16384 | tf_op jit(solution)/shard_map/all_to_all | solution.py:132
  32.4 8.6 %all_gather.7 = bf16[1,256,1024]{2,1,0:T(8,128)(2,1)S(1)} all-gather(bf16[1,256,512]{2,1,0:T(8,128)(2,1)} %param.13), channel_id=1, replica_groups=mesh['groups'=2,'ctx'=4,'tensor'=2,'dp'=2] {'tensor'}, dimensions={2}, use_global_device_ids=true | all-gather | bytes 786432 | tf_op jit(solution)/shard_map/all_gather | solution.py:88
  42.4 3.4 scatter_custom_fusion.2
  45.8 0.9 copy.80
  46.8 4.8 %all-to-all-start.3 = ((bf16[4,4,192,128]{3,2,0,1:T(8,128)(2,1)}), bf16[4,4,192,128]{3,2,0,1:T(8,128)(2,1)}, u32[]{:S(2)}, u32[]{:S(2)}) async-start(bf16[4,4,192,128]{3,2,0,1:T(8,128)(2,1)} %copy.80), calls=%async_computation.4 | async-start | bytes 1572864 | tf_op jit(solution)/shard_map/all_to_all | solution.py:148
  51.6 4.7 %copy.69 = bf16[1024,3,512]{0,2,1:T(8,128)(2,1)} copy(bf16[1024,3,512]{2,0,1:T(8,128)(2,1)} %param.10) | data formatting | bytes 6291456 | tf_op args[1]
  56.3 7.0 %all_gather.6 = bf16[1,256,1024]{2,1,0:T(8,128)(2,1)S(1)} all-gather(bf16[1,256,512]{2,1,0:T(8,128)(2,1)S(1)} %copy-done.10), channel_id=1, replica_groups=mesh['groups'=2,'ctx'=4,'tensor'=2,'dp'=2] {'tensor'}, dimensions={2}, use_global_device_ids=true | all-gather | bytes 786432 | tf_op jit(solution)/shard_map/all_gather | solution.py:87
  64.1 2.9 convolution_convert_fusion.2
  68.2 1.2 copy.71
  69.3 6.5 %scatter_custom_fusion.1 = bf16[3072,384]{1,0:T(8,128)(2,1)S(1)} fusion(s32[1024]{0:T(1024)S(1)} %bitcast.230, bf16[1024,384]{1,0:T(8,128)(2,1)} %copy.71, bf16[]{:T(256)} %constant.102.clone.1), kind=kCustom, calls=%fused_computation.77 | custom fusion | bytes 2359808
  75.8 1.7 copy.72
  77.5 5.1 %all-to-all-start.1 = ((bf16[4,4,192,384]{3,2,0,1:T(8,128)(2,1)}), bf16[4,4,192,384]{3,2,0,1:T(8,128)(2,1)}, u32[]{:S(2)}, u32[]{:S(2)}) async-start(bf16[4,4,192,384]{3,2,0,1:T(8,128)(2,1)} %copy.72), calls=%async_computation.1 | async-start | bytes 4718592 | tf_op jit(solution)/shard_map/all_to_all | solution.py:131
  82.9 2.1 copy.81
  85.0 48.7 %all-to-all-done.1 = bf16[4,4,192,384]{3,2,0,1:T(8,128)(2,1)} async-done(((bf16[4,4,192,384]{3,2,0,1:T(8,128)(2,1)}), bf16[4,4,192,384]{3,2,0,1:T(8,128)(2,1)}, u32[]{:S(2)}, u32[]{:S(2)}) %all-to-all-start.1) | async-done | bytes 2359328 | tf_op jit(solution)/shard_map/all_to_all | solution.py:131
  133.7 1.9 copy.73
  135.6 1.6 fusion.105
  137.4 23.0 %while.33 = (s32[]{:T(128)}, bf16[3,4,256,128]{3,2,0,1:T(8,128)(2,1)S(1)}, s32[3]{0:T(128)S(1)}, bf16[4,768]{1,0:T(4,128)(2,1)S(1)}, bf16[4,4,192]{2,1,0:T(4,128...) while((s32[]{:T(128)}, ...), condition=%wide.wide.region_8.9_spmd, body=%wide.wide.region_5.8_spmd.sunk | while | flops 612764160 | bytes 3175139 | solution.py:43
  138.8 2.5 fusion.172
  141.3 3.8 fusion.173
  146.5 2.5 fusion.172
  149.0 3.8 fusion.173
  154.1 2.5 fusion.172
  156.6 3.8 fusion.173
  161.4 4.2 all-to-all-start.2
  165.6 1.1 broadcast.146.clone
  166.7 56.3 %while.34 = (s32[]{:T(128)}, f32[4,768,128]{2,1,0:T(8,128)S(1)}, f32[4,768,128]{2,1,0:T(8,128)}, bf16[3,4,256,128]{3,2,0,1:T(8,128)(2,1)}, s32[3]{0:T(128)S(1)},...) while((s32[]{:T(128)}, f32[4,768,128]{2,1,0:T(8,128)S(1)}, ...), condition=%wide.wide.region_15.16_spmd.clone, body=%wide.wide.region_11.15_spmd.clone.sunk | while | flops 1222772224 | bytes 25732404 | solution.py:75
  168.0 1.2 fusion.186
  169.2 4.1 fusion.187
  173.3 3.0 multiply_convert_fusion.3
  176.4 1.3 fusion.188
  177.6 2.2 select_add_fusion.6
  179.9 5.2 %select_add_fusion.7 = f32[4,768,128]{2,1,0:T(8,128)} fusion(f32[4,768,128]{2,1,0:T(8,128)} %get-tuple-element.590, f32[4,256]{1,0:T(4,128)S(1)} %get-tuple-element.527, pred[]{:T(512)S(6)} %compare.29, bf16[4,768,128]{2,1,0:T(8,128)(2,1)} %get-tuple-element.615, s32[]{:T(128)S(1)} %bitcast.226, ...), kind=kOutput, calls=%fused_computation.37.clone.clone.1 | convolution fusion | flops 408160000 | bytes 4469761 | tf_op jit(solution)/shard_map/vmap()/while/body/eval_jaxpr/dot_general | solution.py:17
  186.4 1.2 fusion.186
  187.6 4.1 fusion.187
  191.7 3.0 multiply_convert_fusion.3
  194.8 1.3 fusion.188
  196.0 2.2 select_add_fusion.6
  198.3 5.7 %select_add_fusion.7 = f32[4,768,128]{2,1,0:T(8,128)} fusion(f32[4,768,128]{2,1,0:T(8,128)} %get-tuple-element.590, f32[4,256]{1,0:T(4,128)S(1)} %get-tuple-element.527, pred[]{:T(512)S(6)} %compare.29, bf16[4,768,128]{2,1,0:T(8,128)(2,1)} %get-tuple-element.615, s32[]{:T(128)S(1)} %bitcast.226, ...), kind=kOutput, calls=%fused_computation.37.clone.clone.1 | convolution fusion | flops 408160000 | bytes 4469761 | tf_op jit(solution)/shard_map/vmap()/while/body/eval_jaxpr/dot_general | solution.py:17
  205.3 1.2 fusion.186
  206.6 4.1 fusion.187
  210.7 3.0 multiply_convert_fusion.3
  213.7 1.3 fusion.188
  215.0 2.2 select_add_fusion.6
  217.2 5.7 %select_add_fusion.7 = f32[4,768,128]{2,1,0:T(8,128)} fusion(f32[4,768,128]{2,1,0:T(8,128)} %get-tuple-element.590, f32[4,256]{1,0:T(4,128)S(1)} %get-tuple-element.527, pred[]{:T(512)S(6)} %compare.29, bf16[4,768,128]{2,1,0:T(8,128)(2,1)} %get-tuple-element.615, s32[]{:T(128)S(1)} %bitcast.226, ...), kind=kOutput, calls=%fused_computation.37.clone.clone.1 | convolution fusion | flops 408160000 | bytes 4469761 | tf_op jit(solution)/shard_map/vmap()/while/body/eval_jaxpr/dot_general | solution.py:17
  223.1 1.3 copy-done.8
  224.5 1.5 pad_maximum_fusion
  226.0 1.7 copy.84
  227.6 5.2 %all-to-all-start.4 = ((bf16[4,4,192,384]{3,2,0,1:T(8,128)(2,1)}), bf16[4,4,192,384]{3,2,0,1:T(8,128)(2,1)}, u32[]{:S(2)}, u32[]{:S(2)}) async-start(bf16[4,4,192,384]{3,2,0,1:T(8,128)(2,1)} %copy.84), calls=%async_computation.5 | async-start | bytes 4718592 | tf_op jit(solution)/shard_map/all_to_all | solution.py:156
  232.9 1.2 copy.77
  234.1 5.8 %gather_fusion = bf16[1024,128]{1,0:T(8,128)(2,1)S(1)} fusion(bf16[4,768,128]{2,1,0:T(8,128)(2,1)S(1)} %bitcast.205, s32[1024]{0:T(1024)S(1)} %bitcast.199), kind=kCustom, calls=%fused_computation | custom fusion | bytes 532480 | tf_op jit(solution)/shard_map/vmap(jit(_take))/gather | solution.py:123
  240.9 1.4 convolution_convert_fusion.3
  242.3 43.4 %all-to-all-done.4 = bf16[4,4,192,384]{3,2,0,1:T(8,128)(2,1)} async-done(((bf16[4,4,192,384]{3,2,0,1:T(8,128)(2,1)}), bf16[4,4,192,384]{3,2,0,1:T(8,128)(2,1)}, u32[]{:S(2)}, u32[]{:S(2)}) %all-to-all-start.4) | async-done | bytes 2359328 | tf_op jit(solution)/shard_map/all_to_all | solution.py:156
  285.7 1.9 copy.85
  287.6 11.6 %gather_fusion.1 = bf16[1024,384]{1,0:T(8,128)(2,1)} fusion(bf16[4,768,384]{2,1,0:T(8,128)(2,1)S(1)} %bitcast.201, s32[1024]{0:T(1024)S(1)} %bitcast.200), kind=kCustom, calls=%fused_computation.1 | custom fusion | bytes 1581056 | tf_op jit(solution)/shard_map/vmap(jit(_take))/gather | solution.py:123
  299.2 1.5 copy.86
  301.7 2.7 convolution_convert_fusion.1
  304.4 4.7 %copy.88 = bf16[1024,3,512]{2,0,1:T(8,128)(2,1)} copy(bf16[1024,3,512]{0,2,1:T(8,128)(2,1)} %bitcast.202) | data formatting | bytes 6291456 | tf_op jit(solution)/shard_map/convert_element_type | solution.py:168
  310.0 1.3 convolution_convert_fusion.4
  311.3 3.7 convolution_convert_fusion.5
  315.1 90.2 %all-reduce.3.cloned.1.call-done = (bf16[1024,3,512]{2,0,1:T(8,128)(2,1)}, bf16[512,1024]{1,0:T(8,128)(2,1)}) async-done(((bf16[1024,3,512]{2,0,1:T(8,128)(2,1)}, bf16[512,1024]{1,0:T(8,128)(2,1)}), (bf16[1024,3,512]{2,0,1:T(8,128)(2,1)}, bf16[512,1024]{1,0:T(8,128)(2,1)})) %all-reduce.3.cloned.1.call-update) | async-done | bytes 4194320 | tf_op jit(solution)/shard_map/psum | solution.py:168
  405.3 2.9 convert_element_type.81
  408.2 3.6 convert_element_type.79
  (104 shorter events, 17.5 us)
Async XLA Ops:
  8.0 33.8 %copy-start = (bf16[512,1024]{1,0:T(8,128)(2,1)S(1)}, bf16[512,1024]{1,0:T(8,128)(2,1)}, u32[]{:S(2)}) copy-start(bf16[512,1024]{1,0:T(8,128)(2,1)} %param.11) | copy-start | bytes 3145732
  26.1 20.7 %all-to-all-start = ((bf16[4,4,192]{2,0,1:T(4,128)(2,1)}), bf16[4,4,192]{2,0,1:T(4,128)(2,1)S(1)}, u32[]{:S(2)}, u32[]{:S(2)}) async-start(bf16[4,4,192]{2,0,1:T(4,128)(2,1)} %copy.67), calls=%async_computation | async-start | bytes 16384 | tf_op jit(solution)/shard_map/all_to_all | solution.py:132
  41.0 0.8 copy-start.1
  46.8 30.7 %all-to-all-start.3 = ((bf16[4,4,192,128]{3,2,0,1:T(8,128)(2,1)}), bf16[4,4,192,128]{3,2,0,1:T(8,128)(2,1)}, u32[]{:S(2)}, u32[]{:S(2)}) async-start(bf16[4,4,192,128]{3,2,0,1:T(8,128)(2,1)} %copy.80), calls=%async_computation.4 | async-start | bytes 1572864 | tf_op jit(solution)/shard_map/all_to_all | solution.py:148
  51.6 4.7 %copy-start.10 = (bf16[1,256,512]{2,1,0:T(8,128)(2,1)S(1)}, bf16[1,256,512]{2,1,0:T(8,128)(2,1)}, u32[]{:S(2)}) copy-start(bf16[1,256,512]{2,1,0:T(8,128)(2,1)} %param.9) | copy-start | bytes 786436
  63.3 0.8 copy-start.6
  77.5 56.2 %all-to-all-start.1 = ((bf16[4,4,192,384]{3,2,0,1:T(8,128)(2,1)}), bf16[4,4,192,384]{3,2,0,1:T(8,128)(2,1)}, u32[]{:S(2)}, u32[]{:S(2)}) async-start(bf16[4,4,192,384]{3,2,0,1:T(8,128)(2,1)} %copy.72), calls=%async_computation.1 | async-start | bytes 4718592 | tf_op jit(solution)/shard_map/all_to_all | solution.py:131
  82.6 53.0 %copy-start.11 = (bf16[4,4,192]{2,1,0:T(4,128)(2,1)}, bf16[4,4,192]{2,1,0:T(4,128)(2,1)S(1)}, u32[]{:S(2)}) copy-start(bf16[4,4,192]{2,1,0:T(4,128)(2,1)S(1)} %copy.68) | copy-start | bytes 18436
  161.4 66.2 %all-to-all-start.2 = ((bf16[4,4,192,128]{3,2,0,1:T(8,128)(2,1)}), bf16[4,4,192,128]{3,2,0,1:T(8,128)(2,1)}, u32[]{:S(2)}, u32[]{:S(2)}) async-start(bf16[4,4,192,128]{3,2,0,1:T(8,128)(2,1)} %copy.76), calls=%async_computation.2 | async-start | bytes 1572864 | tf_op jit(solution)/shard_map/all_to_all | solution.py:140
  173.3 3.0 copy-start.9
  191.7 3.0 copy-start.9
  210.7 3.0 copy-start.9
  223.0 1.4 copy-start.8
  227.6 5.2 %copy-start.12 = (s32[1,4,256]{2,1,0:T(4,128)S(1)}, s32[1,4,256]{2,1,0:T(4,128)}, u32[]{:S(2)}) copy-start(s32[1,4,256]{2,1,0:T(4,128)} %param.12) | copy-start | bytes 12292
  227.6 58.0 %all-to-all-start.4 = ((bf16[4,4,192,384]{3,2,0,1:T(8,128)(2,1)}), bf16[4,4,192,384]{3,2,0,1:T(8,128)(2,1)}, u32[]{:S(2)}, u32[]{:S(2)}) async-start(bf16[4,4,192,384]{3,2,0,1:T(8,128)(2,1)} %copy.84), calls=%async_computation.5 | async-start | bytes 4718592 | tf_op jit(solution)/shard_map/all_to_all | solution.py:156
  232.8 8.0 %copy-start.2 = (bf16[1,256,1024]{2,1,0:T(8,128)(2,1)S(1)}, bf16[1,256,1024]{2,1,0:T(8,128)(2,1)}, u32[]{:S(2)}) copy-start(bf16[1,256,1024]{2,1,0:T(8,128)(2,1)} %copy-done.1) | copy-start | bytes 1572868
  232.8 172.4 %all-reduce.3.cloned.1.call-start = ((), (), s32[]{:S(2)}) async-start(), calls=%async_computation.9 | async-start | bytes 8388608 | tf_op jit(solution)/shard_map/psum | solution.py:168
  240.2 0.7 copy-start.4
  299.2 2.5 copy-start.7
  309.1 0.9 copy-start.5
  309.1 102.7 %reduce-scatter.3.cloned.1.call-start = ((), (), s32[]{:S(2)}) async-start(), calls=%async_computation.7 | async-start | bytes 786432 | tf_op jit(solution)/shard_map/reduce_scatter | solution.py:160
  311.3 100.5 %reduce-scatter.5.cloned.1.call-start = ((), (), s32[]{:S(2)}) async-start(), calls=%async_computation.8 | async-start | bytes 786432 | tf_op jit(solution)/shard_map/reduce_scatter | solution.py:172
  405.2 2.9 copy-start.3
Sparse Core Ops, SparseCore 0:
  309.2 95.9 all-reduce.2
Sparse Core Ops, SparseCore 1:
  312.4 13.6 reduce-scatter.2
  328.8 14.5 reduce-scatter.4
where the time goes:
time: 421 us; the launch traced here: 419 us
  waiting for transfers between devices  182 us (43%)
  matrix products  80 us (19%)
  local copies, waits for them, and re-layouts  74.3 us (18%)
  starting transfers between devices  25.7 us (6%)
  other arithmetic  21.4 us (5%)
  between operations  15.8 us (4%)
  blocking collectives  15.7 us (4%)
    psum x1, waiting for transfers between devices, shards(): lax.psum(grad_w_qkv_local.astype(jnp.bfloat16), ('ctx', 'dp'))  90.2 us
    all_to_all x1, waiting for transfers between devices, shards(): lax.all_to_all(pack(qkv_heads), 'ctx', split_axis=1, concat_axis=1, tiled...  48.7 us
    all_to_all x1, waiting for transfers between devices, shards(): lax.all_to_all(grads_own, 'ctx', split_axis=1, concat_axis=1, tiled=True)  43.4 us
    dot_general x8, matrix products, contract_first(): lax.dot_general(left, right, (((0,), (0,)), ((), ())), preferred_element_...  27.5 us
    unnamed x32, local copies, waits for them, and re-layouts  26.9 us
    sub x6, matrix products, masked_probs(): expo = jnp.exp(scores - top_value)  19.8 us
    gather x5, local copies, waits for them, and re-layouts, unpack(): jnp.take(table, where_to, axis=0)  19.6 us
    dot_general x5, matrix products, contract_last(): lax.dot_general(left, right, (((1,), (1,)), ((), ())), preferred_element_...  13.2 us
  transfers between devices with their start and end apart: 8, of which 3 were waited for; matrix products, arithmetic and copies ran while one was open for 25% of the time, Pallas kernels for 0%

commit v1 on v0

--- a/solution.py
+++ b/solution.py
@@ -5,6 +5,7 @@
 from jax.sharding import PartitionSpec as P
 
 HD = 128
+run_the_waves = lambda sample: lax.psum(lax.psum(sample, "dp"), "ctx")
 
 
 def contract_last(left, right):
@@ -165,7 +166,7 @@
     grad_w_out_local = contract_first(attention_rows, tok_grads)
     grad_w_qkv_local = contract_first(tok_rows, grad_qkv).reshape(width, 3, heads_local * HD)
     summed_qkv, summed_out = (
-        lax.psum(grad_w_qkv_local.astype(jnp.bfloat16), ("ctx", "dp")).astype(jnp.float32),
+        run_the_waves(grad_w_qkv_local.astype(jnp.bfloat16)).astype(jnp.float32),
         lax.psum(grad_w_out_local.astype(jnp.bfloat16), ("ctx", "dp")).astype(jnp.float32),
     )
     in_terms = contract_last(grad_qkv, w_qkv.reshape(width, 3 * heads_local * HD))

time: 421 us -> 530 us (1.26)
  waiting for transfers between devices: 182 us -> 275 us
  blocking collectives: 15.7 us -> 37.7 us
    psum x1 -> x3, waiting for transfers between devices: 90.2 us -> 172 us  [the longest x2 120 us: run_the_waves = lambda sample: lax.psum(lax.psum(sample, 'dp'), 'ctx')]
    all_to_all x0 -> x1, blocking collectives: none -> 22.1 us  [shards(): lax.all_to_all(attention_own.reshape(heads_local, ctx_count, capacity, HD...]
    all_to_all x1, waiting for transfers between devices: 43.4 us -> 53.1 us  [shards(): lax.all_to_all(grads_own, 'ctx', split_axis=1, concat_axis=1, tiled=True)]
    unnamed x32 -> x30, local copies, waits for them, and re-layouts: 26.9 us -> 26.7 us
  transfers between devices with their start and end apart: 8 -> 9, of which waited for: 3 -> 4; matrix products, arithmetic and copies ran while one was open for 25% -> 9% of each run, Pallas kernels for 0% -> 0%
where the time goes in v1:
time: 530 us; the launch traced here: 528 us
  waiting for transfers between devices  275 us (52%)
  matrix products  79.9 us (15%)
  local copies, waits for them, and re-layouts  72.2 us (14%)
  blocking collectives  37.7 us (7%)
  other arithmetic  23.1 us (4%)
  starting transfers between devices  21.3 us (4%)
  between operations  15.5 us (3%)
    psum x2, waiting for transfers between devices, run_the_waves = lambda sample: lax.psum(lax.psum(sample, 'dp'), 'ctx')  120 us
    all_to_all x1, waiting for transfers between devices, shards(): lax.all_to_all(grads_own, 'ctx', split_axis=1, concat_axis=1, tiled=True)  53.1 us
    psum x1, waiting for transfers between devices, shards(): lax.psum(grad_w_out_local.astype(jnp.bfloat16), ('ctx', 'dp'))  52.2 us
    all_to_all x1, waiting for transfers between devices, shards(): lax.all_to_all(pack(qkv_heads), 'ctx', split_axis=1, concat_axis=1, tiled...  48.8 us
    dot_general x8, matrix products, contract_first(): lax.dot_general(left, right, (((0,), (0,)), ((), ())), preferred_element_...  27.4 us
    unnamed x30, local copies, waits for them, and re-layouts  26.7 us
    all_to_all x1, blocking collectives, shards(): lax.all_to_all(attention_own.reshape(heads_local, ctx_count, capacity, HD...  22.1 us
    sub x6, matrix products, masked_probs(): expo = jnp.exp(scores - top_value)  19.8 us
  transfers between devices with their start and end apart: 9, of which 4 were waited for; matrix products, arithmetic and copies ran while one was open for 9% of the time, Pallas kernels for 0%

profile of v1, /device:TPU:0, one launch (start us, length us, event | category | flops | bytes accessed | tf_op | source)
XLA Modules:
  0.0 528.3 jit_solution(6833130238845513944)
XLA Ops:
  10.2 4.8 reduce-window.6
  17.8 7.6 %scatter_custom_fusion = bf16[3072]{0:T(1024)(128)(2,1)S(1)} fusion(s32[1024]{0:T(1024)S(1)} %bitcast.228, bf16[1024]{0:T(1024)(128)(2,1)S(1)} %bitcast.231, bf16[]{:T(256)} %constant.103.clone.1), kind=kCustom, calls=%fused_computation.120 | custom fusion | bytes 6146
  26.1 6.3 %all-to-all-start = ((bf16[4,4,192]{2,0,1:T(4,128)(2,1)}), bf16[4,4,192]{2,0,1:T(4,128)(2,1)S(1)}, u32[]{:S(2)}, u32[]{:S(2)}) async-start(bf16[4,4,192]{2,0,1:T(4,128)(2,1)} %copy.67), calls=%async_computation | async-start | bytes 16384 | tf_op jit(solution)/shard_map/all_to_all | solution.py:133
  32.4 8.6 %all_gather.7 = bf16[1,256,1024]{2,1,0:T(8,128)(2,1)S(1)} all-gather(bf16[1,256,512]{2,1,0:T(8,128)(2,1)} %param.13), channel_id=1, replica_groups=mesh['groups'=2,'ctx'=4,'tensor'=2,'dp'=2] {'tensor'}, dimensions={2}, use_global_device_ids=true | all-gather | bytes 786432 | tf_op jit(solution)/shard_map/all_gather | solution.py:89
  42.4 3.4 scatter_custom_fusion.2
  46.8 4.8 all-to-all-start.3
  51.6 4.7 copy.69
  56.3 7.0 %all_gather.6 = bf16[1,256,1024]{2,1,0:T(8,128)(2,1)S(1)} all-gather(bf16[1,256,512]{2,1,0:T(8,128)(2,1)S(1)} %copy-done.9), channel_id=1, replica_groups=mesh['groups'=2,'ctx'=4,'tensor'=2,'dp'=2] {'tensor'}, dimensions={2}, use_global_device_ids=true | all-gather | bytes 786432 | tf_op jit(solution)/shard_map/all_gather | solution.py:88
  64.1 2.9 convolution_convert_fusion.2
  68.2 1.2 copy.71
  69.3 6.5 %scatter_custom_fusion.1 = bf16[3072,384]{1,0:T(8,128)(2,1)S(1)} fusion(s32[1024]{0:T(1024)S(1)} %bitcast.230, bf16[1024,384]{1,0:T(8,128)(2,1)} %copy.71, bf16[]{:T(256)} %constant.102.clone.1), kind=kCustom, calls=%fused_computation.77 | custom fusion | bytes 2359808
  75.8 1.7 copy.72
  77.5 5.1 all-to-all-start.1
  82.9 2.1 copy.81
  85.0 48.8 %all-to-all-done.1 = bf16[4,4,192,384]{3,2,0,1:T(8,128)(2,1)} async-done(((bf16[4,4,192,384]{3,2,0,1:T(8,128)(2,1)}), bf16[4,4,192,384]{3,2,0,1:T(8,128)(2,1)}, u32[]{:S(2)}, u32[]{:S(2)}) %all-to-all-start.1) | async-done | bytes 2359328 | tf_op jit(solution)/shard_map/all_to_all | solution.py:132
  133.7 1.9 copy.73
  135.6 1.6 fusion.105
  137.4 23.1 %while.33 = (s32[]{:T(128)}, bf16[3,4,256,128]{3,2,0,1:T(8,128)(2,1)S(1)}, s32[3]{0:T(128)S(1)}, bf16[4,768]{1,0:T(4,128)(2,1)S(1)}, bf16[4,4,192]{2,1,0:T(4,128...) while((s32[]{:T(128)}, ...), condition=%wide.wide.region_8.9_spmd, body=%wide.wide.region_5.8_spmd.sunk | while | flops 612764160 | bytes 3175139 | solution.py:44
  138.8 2.5 fusion.172
  141.3 3.8 fusion.173
  146.5 2.5 fusion.172
  149.0 3.8 fusion.173
  154.3 2.5 fusion.172
  156.8 3.8 fusion.173
  160.6 1.0 broadcast.146.clone
  161.6 56.3 %while.34 = (s32[]{:T(128)}, f32[4,768,128]{2,1,0:T(8,128)S(1)}, f32[4,768,128]{2,1,0:T(8,128)}, bf16[3,4,256,128]{3,2,0,1:T(8,128)(2,1)}, s32[3]{0:T(128)S(1)},...) while((s32[]{:T(128)}, f32[4,768,128]{2,1,0:T(8,128)S(1)}, ...), condition=%wide.wide.region_15.16_spmd.clone, body=%wide.wide.region_11.15_spmd.clone.sunk | while | flops 1222772224 | bytes 25732404 | solution.py:76
  162.9 1.2 fusion.186
  164.2 4.1 fusion.187
  168.3 3.0 multiply_convert_fusion.3
  171.3 1.3 fusion.188
  172.6 2.2 select_add_fusion.6
  174.8 5.2 select_add_fusion.7
  181.4 1.2 fusion.186
  182.6 4.1 fusion.187
  186.7 3.0 multiply_convert_fusion.3
  189.7 1.3 fusion.188
  191.0 2.2 select_add_fusion.6
  193.2 5.7 %select_add_fusion.7 = f32[4,768,128]{2,1,0:T(8,128)} fusion(f32[4,768,128]{2,1,0:T(8,128)} %get-tuple-element.588, f32[4,256]{1,0:T(4,128)S(1)} %get-tuple-element.525, pred[]{:T(512)S(6)} %compare.29, bf16[4,768,128]{2,1,0:T(8,128)(2,1)} %get-tuple-element.613, s32[]{:T(128)S(1)} %bitcast.226, ...), kind=kOutput, calls=%fused_computation.37.clone.clone.1 | convolution fusion | flops 408160000 | bytes 4469761 | tf_op jit(solution)/shard_map/vmap()/while/body/eval_jaxpr/dot_general | solution.py:18
  200.3 1.2 fusion.186
  201.5 4.1 fusion.187
  205.6 3.0 multiply_convert_fusion.3
  208.7 1.3 fusion.188
  209.9 2.2 select_add_fusion.6
  212.2 5.7 %select_add_fusion.7 = f32[4,768,128]{2,1,0:T(8,128)} fusion(f32[4,768,128]{2,1,0:T(8,128)} %get-tuple-element.588, f32[4,256]{1,0:T(4,128)S(1)} %get-tuple-element.525, pred[]{:T(512)S(6)} %compare.29, bf16[4,768,128]{2,1,0:T(8,128)(2,1)} %get-tuple-element.613, s32[]{:T(128)S(1)} %bitcast.226, ...), kind=kOutput, calls=%fused_computation.37.clone.clone.1 | convolution fusion | flops 408160000 | bytes 4469761 | tf_op jit(solution)/shard_map/vmap()/while/body/eval_jaxpr/dot_general | solution.py:18
  218.0 1.6 copy-done.7
  219.7 1.5 pad_maximum_fusion
  221.2 1.6 copy.84
  222.8 4.6 all-to-all-start.4
  227.8 53.1 %all-to-all-done.4 = bf16[4,4,192,384]{3,2,0,1:T(8,128)(2,1)} async-done(((bf16[4,4,192,384]{3,2,0,1:T(8,128)(2,1)}), bf16[4,4,192,384]{3,2,0,1:T(8,128)(2,1)}, u32[]{:S(2)}, u32[]{:S(2)}) %all-to-all-start.4) | async-done | bytes 2359328 | tf_op jit(solution)/shard_map/all_to_all | solution.py:157
  280.8 1.9 copy.85
  282.7 11.6 %gather_fusion.1 = bf16[1024,384]{1,0:T(8,128)(2,1)} fusion(bf16[4,768,384]{2,1,0:T(8,128)(2,1)S(1)} %bitcast.201, s32[1024]{0:T(1024)S(1)} %bitcast.199), kind=kCustom, calls=%fused_computation.1 | custom fusion | bytes 1581056 | tf_op jit(solution)/shard_map/vmap(jit(_take))/gather | solution.py:124
  294.4 1.5 copy.86
  296.9 2.7 convolution_convert_fusion.1
  299.6 4.7 copy.88
  304.3 1.1 copy-done.2
  305.5 22.1 %all_to_all.25 = bf16[4,4,192,128]{3,2,0,1:T(8,128)(2,1)S(1)} all-to-all(bf16[4,4,192,128]{3,2,0,1:T(8,128)(2,1)S(1)} %copy.76), channel_id=1, replica_groups=mesh['groups'=2,'ctx'=4,'tensor'=2,'dp'=2] {'ctx'}, dimensions={1} | all-to-all | bytes 1572864 | tf_op jit(solution)/shard_map/all_to_all | solution.py:141
  327.6 5.8 %gather_fusion = bf16[1024,128]{1,0:T(8,128)(2,1)S(1)} fusion(bf16[4,768,128]{2,1,0:T(8,128)(2,1)S(1)} %bitcast.205, s32[1024]{0:T(1024)S(1)} %bitcast.200), kind=kCustom, calls=%fused_computation | custom fusion | bytes 532480 | tf_op jit(solution)/shard_map/vmap(jit(_take))/gather | solution.py:124
  333.6 1.4 convolution_convert_fusion.3
  335.8 1.3 convolution_convert_fusion.4
  337.2 3.7 convolution_convert_fusion.5
  340.9 52.2 %all-reduce.8.cloned.1.call-done = bf16[512,1024]{1,0:T(8,128)(2,1)} async-done(((bf16[512,1024]{1,0:T(8,128)(2,1)}), bf16[512,1024]{1,0:T(8,128)(2,1)}) %all-reduce.8.cloned.1.call-update) | async-done | bytes 1048592 | tf_op jit(solution)/shard_map/psum | solution.py:170
  393.1 2.8 convert_element_type.81
  395.9 119.8 %all-reduce.6.cloned.1.call-done = bf16[1024,3,512]{2,0,1:T(8,128)(2,1)} async-done(((bf16[1024,3,512]{2,0,1:T(8,128)(2,1)}), bf16[1024,3,512]{2,0,1:T(8,128)(2,1)}) %all-reduce.6.cloned.1.call-update) | async-done | bytes 3145744 | tf_op jit(solution)/shard_map/psum | solution.py:8
  515.7 5.5 %convert_element_type.79 = f32[1024,3,512]{2,0,1:T(8,128)} convert(bf16[1024,3,512]{2,0,1:T(8,128)(2,1)} %all-reduce.6.cloned.1.call-done) | non-fusion elementwise | flops 1572864 | bytes 9437184 | tf_op jit(solution)/shard_map/convert_element_type | solution.py:169
  (107 shorter events, 17.2 us)
Async XLA Ops:
  8.0 33.8 %copy-start = (bf16[512,1024]{1,0:T(8,128)(2,1)S(1)}, bf16[512,1024]{1,0:T(8,128)(2,1)}, u32[]{:S(2)}) copy-start(bf16[512,1024]{1,0:T(8,128)(2,1)} %param.11) | copy-start | bytes 3145732
  26.1 20.7 %all-to-all-start = ((bf16[4,4,192]{2,0,1:T(4,128)(2,1)}), bf16[4,4,192]{2,0,1:T(4,128)(2,1)S(1)}, u32[]{:S(2)}, u32[]{:S(2)}) async-start(bf16[4,4,192]{2,0,1:T(4,128)(2,1)} %copy.67), calls=%async_computation | async-start | bytes 16384 | tf_op jit(solution)/shard_map/all_to_all | solution.py:133
  41.0 0.8 copy-start.3
  46.8 30.7 %all-to-all-start.3 = ((bf16[4,4,192,128]{3,2,0,1:T(8,128)(2,1)}), bf16[4,4,192,128]{3,2,0,1:T(8,128)(2,1)}, u32[]{:S(2)}, u32[]{:S(2)}) async-start(bf16[4,4,192,128]{3,2,0,1:T(8,128)(2,1)} %copy.80), calls=%async_computation.4 | async-start | bytes 1572864 | tf_op jit(solution)/shard_map/all_to_all | solution.py:149
  51.6 4.7 copy-start.9
  63.3 0.8 copy-start.5
  77.5 56.2 %all-to-all-start.1 = ((bf16[4,4,192,384]{3,2,0,1:T(8,128)(2,1)}), bf16[4,4,192,384]{3,2,0,1:T(8,128)(2,1)}, u32[]{:S(2)}, u32[]{:S(2)}) async-start(bf16[4,4,192,384]{3,2,0,1:T(8,128)(2,1)} %copy.72), calls=%async_computation.1 | async-start | bytes 4718592 | tf_op jit(solution)/shard_map/all_to_all | solution.py:132
  82.6 53.0 %copy-start.10 = (bf16[4,4,192]{2,1,0:T(4,128)(2,1)}, bf16[4,4,192]{2,1,0:T(4,128)(2,1)S(1)}, u32[]{:S(2)}) copy-start(bf16[4,4,192]{2,1,0:T(4,128)(2,1)S(1)} %copy.68) | copy-start | bytes 18436
  168.3 3.0 copy-start.8
  186.7 3.0 copy-start.8
  205.6 3.0 copy-start.8
  217.9 3.3 copy-start.1
  217.9 1.7 copy-start.7
  222.8 4.9 copy-start.11
  222.8 58.0 %all-to-all-start.4 = ((bf16[4,4,192,384]{3,2,0,1:T(8,128)(2,1)}), bf16[4,4,192,384]{3,2,0,1:T(8,128)(2,1)}, u32[]{:S(2)}, u32[]{:S(2)}) async-start(bf16[4,4,192,384]{3,2,0,1:T(8,128)(2,1)} %copy.84), calls=%async_computation.5 | async-start | bytes 4718592 | tf_op jit(solution)/shard_map/all_to_all | solution.py:157
  227.5 107.7 %all-reduce.4.cloned.1.call-start = ((), (), s32[]{:S(2)}) async-start(), calls=%async_computation.9 | async-start | bytes 6291456 | tf_op jit(solution)/shard_map/psum | solution.py:8
  294.4 2.5 copy-start.6
  304.3 1.1 copy-start.2
  304.3 88.8 %all-reduce.8.cloned.1.call-start = ((), (), s32[]{:S(2)}) async-start(), calls=%async_computation.11 | async-start | bytes 2097152 | tf_op jit(solution)/shard_map/psum | solution.py:170
  327.5 6.1 %copy-start.4 = (bf16[1,256,1024]{2,1,0:T(8,128)(2,1)S(1)}, bf16[1,256,1024]{2,1,0:T(8,128)(2,1)}, u32[]{:S(2)}) copy-start(bf16[1,256,1024]{2,1,0:T(8,128)(2,1)} %copy-done.3) | copy-start | bytes 1572868
  335.1 180.6 %all-reduce.6.cloned.1.call-start = ((), (), s32[]{:S(2)}) async-start(), calls=%async_computation.10 | async-start | bytes 6291456 | tf_op jit(solution)/shard_map/psum | solution.py:8
  335.8 185.4 %reduce-scatter.3.cloned.1.call-start = ((), (), s32[]{:S(2)}) async-start(), calls=%async_computation.7 | async-start | bytes 786432 | tf_op jit(solution)/shard_map/reduce_scatter | solution.py:161
  337.1 184.1 %reduce-scatter.5.cloned.1.call-start = ((), (), s32[]{:S(2)}) async-start(), calls=%async_computation.8 | async-start | bytes 786432 | tf_op jit(solution)/shard_map/reduce_scatter | solution.py:173
Sparse Core Ops, SparseCore 0:
  304.4 22.3 all-reduce.3
  335.2 57.9 all-reduce.7
  395.6 120.0 all-reduce.5
Sparse Core Ops, SparseCore 1:
  339.1 13.5 reduce-scatter.2
  355.4 14.5 reduce-scatter.4
